TPU v7x, 256 devices: a whole 4x4x8 slice. The times are simulated.
256 devices in a mesh: read: 32 (over z_lo, x, core), pos: 8 (over y, z_hi).
Axes of the slice: x: 4, y: 4, z: 8 (z_hi: 2, z_lo: 4; z = z_hi * 4 + z_lo), core: 2. Of those that a mesh axis runs over, the one named last changes fastest.
Arguments:
- features: bfloat16 [128, 256, 768], P('read', 'pos'), may hold values from -6 to 6
- grad_out: bfloat16 [128, 256, 768], P('read', 'pos'), may hold values from -16 to 16
- weights: bfloat16 [4, 768, 768], replicated, may hold values from -0.21875 to 0.21875
- read_start: int32 [128], replicated, may hold values from 0 to 127
- read_end: int32 [128], replicated, may hold values from 129 to 256
Outputs:
- grad_input: bfloat16 [128, 256, 768], P('read', 'pos')
- weight_grads: float32 [768, 3072], P(('read', 'pos'))
Inputs may be any that keep to these rules, and one draw needn't show every extreme that they name: read_end is above read_start for every read.
All inputs are finite; a program needn't handle non-finite values.
Results may differ from a plain program's by a relative error of at most 0.0086.
Values may be sent and summed in bfloat16 or wider, within the bound.
A program may use at most 128 MiB of HBM per device.

v0:
```python
import math
import jax
import jax.numpy as jnp
from jax import lax
from jax.sharding import PartitionSpec as P

HEADS = 12
HEAD_DIM = 64


def coverage(starts, ends, first_col, col_count):
    columns = first_col + jnp.arange(col_count, dtype=jnp.int32)
    inside = (columns[None, :] >= starts[:, None]) & (columns[None, :] < ends[:, None])
    return inside.astype(jnp.float32)


def dot_back(left, right):
    return lax.dot_general(
        left, right, (((1,), (1,)), ((), ())), preferred_element_type=jnp.float32
    )


def project(source, upstream, covered, weights):
    width = source.shape[-1]
    values32 = source.reshape(-1, width).astype(jnp.float32)
    inverse = lax.rsqrt(jnp.mean(values32 * values32, -1, keepdims=True) + 1e-05)
    normed = values32 * inverse
    normed_b = normed.astype(jnp.bfloat16)
    keep_mask = covered.reshape(-1, 1)
    query = (jnp.dot(normed_b, weights[0], preferred_element_type=jnp.float32) * keep_mask).astype(
        jnp.bfloat16
    )
    keys = (jnp.dot(normed_b, weights[1], preferred_element_type=jnp.float32) * keep_mask).astype(
        jnp.bfloat16
    )
    values = (jnp.dot(normed_b, weights[2], preferred_element_type=jnp.float32) * keep_mask).astype(
        jnp.bfloat16
    )
    grad_flat = upstream.reshape(-1, width)
    back_out = dot_back(grad_flat, weights[3]).astype(jnp.bfloat16)
    return (normed, inverse, normed_b, grad_flat, query, keys, values, back_out)


def attend(query, keys, values, back_out, covered, scale):
    reads, narrow, width = query.shape
    shape4 = (reads, narrow, HEADS, HEAD_DIM)
    query4 = query.reshape(shape4)
    keys4 = keys.reshape(shape4)
    values4 = values.reshape(shape4)
    back4 = back_out.reshape(shape4)
    partial_logits = jnp.einsum("rchd,schd->hrs", query4, keys4, preferred_element_type=jnp.float32)
    logits = lax.psum(partial_logits, ("read", "pos")) * scale
    expon = jnp.exp(logits)
    probs = expon / jnp.sum(expon, -1, keepdims=True)
    probs_b = probs.astype(jnp.bfloat16)
    slopes = lax.psum(
        jnp.einsum("rchd,schd->hrs", back4, values4, preferred_element_type=jnp.float32),
        ("read", "pos"),
    )
    mixed = (scale * probs * (slopes - jnp.sum(probs * slopes, -1, keepdims=True))).astype(
        jnp.bfloat16
    )
    output = jnp.einsum(
        "hrs,schd->rchd", probs_b, values4, preferred_element_type=jnp.float32
    ).astype(jnp.bfloat16)
    keep4 = covered[:, :, None, None]
    grad_query = (
        jnp.einsum("hrs,schd->rchd", mixed, keys4, preferred_element_type=jnp.float32) * keep4
    ).astype(jnp.bfloat16)
    grad_keys = (
        jnp.einsum("hrs,rchd->schd", mixed, query4, preferred_element_type=jnp.float32) * keep4
    ).astype(jnp.bfloat16)
    grad_values = (
        jnp.einsum("hrs,rchd->schd", probs_b, back4, preferred_element_type=jnp.float32) * keep4
    ).astype(jnp.bfloat16)
    shape3 = (reads, narrow, width)
    return (
        output.reshape(shape3),
        grad_query.reshape(shape3),
        grad_keys.reshape(shape3),
        grad_values.reshape(shape3),
    )


def input_grad(grad_query, grad_keys, grad_values, weights, normed, inverse):
    grad_norm = (
        dot_back(grad_query, weights[0])
        + dot_back(grad_keys, weights[1])
        + dot_back(grad_values, weights[2])
    )
    result = inverse * (grad_norm - normed * jnp.mean(grad_norm * normed, -1, keepdims=True))
    return result.astype(jnp.bfloat16)


def shards(features, grad_out, weights, read_start, read_end):
    rows, col_dev, width = features.shape
    read_count = lax.axis_size("read")
    pos_count = lax.axis_size("pos")
    read_at = lax.axis_index("read")
    pos_at = lax.axis_index("pos")
    scale = 1.0 / math.sqrt(HEAD_DIM * col_dev * pos_count)
    narrow = col_dev // read_count
    column_first = pos_at * col_dev + read_at * narrow
    column_cover = coverage(read_start, read_end, column_first, narrow)
    starts = lax.dynamic_slice_in_dim(read_start, read_at * rows, rows)
    ends = lax.dynamic_slice_in_dim(read_end, read_at * rows, rows)
    covered = coverage(starts, ends, pos_at * col_dev, col_dev)
    normed, inverse, normed_b, grad_flat, query, keys, values, back_out = project(
        features, grad_out, covered, weights
    )
    token_shape = (rows, col_dev, width)
    col_query, col_keys, col_values, col_back = (
        lax.all_to_all(query.reshape(token_shape), "read", split_axis=1, concat_axis=0, tiled=True),
        lax.all_to_all(keys.reshape(token_shape), "read", split_axis=1, concat_axis=0, tiled=True),
        lax.all_to_all(
            values.reshape(token_shape), "read", split_axis=1, concat_axis=0, tiled=True
        ),
        lax.all_to_all(
            back_out.reshape(token_shape), "read", split_axis=1, concat_axis=0, tiled=True
        ),
    )
    output, grad_query, grad_keys, grad_values = attend(
        col_query, col_keys, col_values, col_back, column_cover, scale
    )
    output, grad_query, grad_keys, grad_values = (
        lax.all_to_all(output, "read", split_axis=0, concat_axis=1, tiled=True),
        lax.all_to_all(grad_query, "read", split_axis=0, concat_axis=1, tiled=True),
        lax.all_to_all(grad_keys, "read", split_axis=0, concat_axis=1, tiled=True),
        lax.all_to_all(grad_values, "read", split_axis=0, concat_axis=1, tiled=True),
    )
    output_flat = output.reshape(-1, width)
    query_flat = grad_query.reshape(-1, width)
    keys_flat = grad_keys.reshape(-1, width)
    values_flat = grad_values.reshape(-1, width)
    grad_input = input_grad(query_flat, keys_flat, values_flat, weights, normed, inverse).reshape(
        token_shape
    )
    right_side = jnp.concatenate([query_flat, keys_flat, values_flat], axis=1)
    inner_part = lax.dot_general(
        normed_b, right_side, (((0,), (0,)), ((), ())), preferred_element_type=jnp.float32
    )
    outer_part = lax.dot_general(
        output_flat, grad_flat, (((0,), (0,)), ((), ())), preferred_element_type=jnp.float32
    )
    weight_grads = lax.psum_scatter(
        jnp.concatenate([inner_part, outer_part], axis=1),
        ("read", "pos"),
        scatter_dimension=0,
        tiled=True,
    )
    return (grad_input, weight_grads)


def solution(mesh):
    in_specs = (P("read", "pos", None), P("read", "pos", None), P(), P(), P())
    out_specs = (P("read", "pos", None), P(("read", "pos"), None))
    return jax.shard_map(shards, mesh=mesh, in_specs=in_specs, out_specs=out_specs, check_vma=False)
```

profile of v0, /device:TPU:97, one launch (start us, length us, event | category | flops | bytes accessed | tf_op | source)
XLA Modules:
  0.0 704.0 jit_solution(4038250459228061290)
XLA Ops:
  11.0 1.6 fusion.16
  13.4 8.0 %all-to-all-start = ((bf16[4,32,768]{2,0,1:T(4,128)(2,1)}), bf16[4,32,768]{2,0,1:T(4,128)(2,1)S(1)}, u32[]{:S(2)}, u32[]{:S(2)}) async-start(bf16[4,32,768]{2,0,1:T(4,128)(2,1)} %copy.33), calls=%async_computation | async-start | bytes 393216 | tf_op jit(solution)/shard_map/all_to_all | solution.py:114
  21.5 1.8 fusion.13
  24.1 5.1 all-to-all-done
  29.2 5.8 all-to-all-start.2
  35.0 1.6 fusion.22
  37.4 5.3 all-to-all-done.2
  42.7 5.8 all-to-all-start.3
  48.5 1.6 fusion.19
  50.9 5.3 all-to-all-done.3
  56.3 5.8 all-to-all-start.1
  64.2 5.6 all-to-all-done.1
  70.5 1.2 fusion.49
  71.7 1.2 fusion.48
  73.0 263.2 %all-reduce.7.cloned.1.call-done = (f32[12,128,128]{2,1,0:T(8,128)}, f32[12,128,128]{2,1,0:T(8,128)}) async-done(((f32[12,128,128]{2,1,0:T(8,128)}, f32[12,128,128]{2,1,0:T(8,128)}), (f32[12,128,128]{2,1,0:T(8,128)}, f32[12,128,128]{2,1,0:T(8,128)})) %all-reduce.7.cloned.1.call-update) | async-done | bytes 1572880 | tf_op jit(solution)/shard_map/psum | solution.py:56
  336.2 1.5 fusion.35
  337.7 1.9 multiply_reduce_fusion
  339.6 1.8 multiply_convert_fusion
  344.0 7.4 %all-to-all-start.4 = ((bf16[32,2,1536]{2,1,0:T(2,128)(2,1)}), bf16[32,2,1536]{2,1,0:T(2,128)(2,1)S(1)}, u32[]{:S(2)}, u32[]{:S(2)}) async-start(bf16[32,2,1536]{2,1,0:T(2,128)(2,1)} %reshape.206), calls=%async_computation.4 | async-start | bytes 393216 | tf_op jit(solution)/shard_map/all_to_all | solution.py:127
  353.4 5.8 all-to-all-done.4
  359.2 5.8 all-to-all-start.5
  367.2 5.6 all-to-all-done.5
  372.8 5.8 all-to-all-start.6
  380.7 5.6 all-to-all-done.6
  386.3 5.8 all-to-all-start.7
  396.4 2.6 fusion.7
  401.7 1.9 convolution_add_fusion.1
  403.6 2.6 fusion.42
  406.2 3.9 fusion.36
  410.2 8.1 %pad_maximum_fusion = f32[768,3072]{1,0:T(8,128)} fusion(f32[768,768]{1,0:T(8,128)S(1)} %fusion.50, f32[768,2304]{1,0:T(8,128)} %fusion.36), kind=kLoop, calls=%fused_computation | loop fusion | flops 2359296 | bytes 18874368 | tf_op jit(solution)/shard_map/concatenate | solution.py:146
  420.1 275.6 %all-reduce.5.cloned.1.call-done = f32[768,3072]{1,0:T(8,128)} async-done(((f32[768,3072]{1,0:T(8,128)}), f32[768,3072]{1,0:T(8,128)}) %all-reduce.5.cloned.1.call-update) | async-done | bytes 9437200
  695.6 1.6 constant_dynamic-slice_fusion
  (75 shorter events, 27.6 us)
Async XLA Ops:
  7.2 14.3 %copy-start = (bf16[4,32,768]{2,1,0:T(8,128)(2,1)S(1)}, bf16[4,32,768]{2,1,0:T(8,128)(2,1)}, u32[]{:S(2)}) copy-start(bf16[4,32,768]{2,1,0:T(8,128)(2,1)} %param.6) | copy-start | bytes 589828
  13.4 15.8 %all-to-all-start = ((bf16[4,32,768]{2,0,1:T(4,128)(2,1)}), bf16[4,32,768]{2,0,1:T(4,128)(2,1)S(1)}, u32[]{:S(2)}, u32[]{:S(2)}) async-start(bf16[4,32,768]{2,0,1:T(4,128)(2,1)} %copy.33), calls=%async_computation | async-start | bytes 393216 | tf_op jit(solution)/shard_map/all_to_all | solution.py:114
  29.2 13.5 %all-to-all-start.2 = ((bf16[4,32,768]{2,0,1:T(4,128)(2,1)}), bf16[4,32,768]{2,0,1:T(4,128)(2,1)S(1)}, u32[]{:S(2)}, u32[]{:S(2)}) async-start(bf16[4,32,768]{2,0,1:T(4,128)(2,1)} %copy.37), calls=%async_computation.2 | async-start | bytes 393216 | tf_op jit(solution)/shard_map/all_to_all | solution.py:118
  42.7 13.5 %all-to-all-start.3 = ((bf16[4,32,768]{2,0,1:T(4,128)(2,1)}), bf16[4,32,768]{2,0,1:T(4,128)(2,1)S(1)}, u32[]{:S(2)}, u32[]{:S(2)}) async-start(bf16[4,32,768]{2,0,1:T(4,128)(2,1)} %copy.38), calls=%async_computation.3 | async-start | bytes 393216 | tf_op jit(solution)/shard_map/all_to_all | solution.py:115
  56.3 13.5 %all-to-all-start.1 = ((bf16[4,32,768]{2,0,1:T(4,128)(2,1)}), bf16[4,32,768]{2,0,1:T(4,128)(2,1)S(1)}, u32[]{:S(2)}, u32[]{:S(2)}) async-start(bf16[4,32,768]{2,0,1:T(4,128)(2,1)} %copy.34), calls=%async_computation.1 | async-start | bytes 393216 | tf_op jit(solution)/shard_map/all_to_all | solution.py:113
  62.0 274.1 %all-reduce.7.cloned.1.call-start = ((), (), s32[]{:S(2)}) async-start(), calls=%async_computation.9 | async-start | bytes 3145728 | tf_op jit(solution)/shard_map/psum | solution.py:56
  62.1 10.9 %copy-start.4 = (s32[128]{0:T(128)S(1)}, s32[128]{0:T(128)}, u32[]{:S(2)}) copy-start(s32[128]{0:T(128)} %param.9) | copy-start | bytes 1540
  62.1 10.9 %copy-start.5 = (s32[128]{0:T(128)S(1)}, s32[128]{0:T(128)}, u32[]{:S(2)}) copy-start(s32[128]{0:T(128)} %param.8) | copy-start | bytes 1540
  336.2 28.8 %copy-start.1 = (f32[12,128,128]{2,1,0:T(8,128)S(1)}, f32[12,128,128]{2,1,0:T(8,128)}, u32[]{:S(2)}) copy-start(f32[12,128,128]{2,1,0:T(8,128)} %get-tuple-element.3) | copy-start | bytes 2359300
  344.0 15.2 %all-to-all-start.4 = ((bf16[32,2,1536]{2,1,0:T(2,128)(2,1)}), bf16[32,2,1536]{2,1,0:T(2,128)(2,1)S(1)}, u32[]{:S(2)}, u32[]{:S(2)}) async-start(bf16[32,2,1536]{2,1,0:T(2,128)(2,1)} %reshape.206), calls=%async_computation.4 | async-start | bytes 393216 | tf_op jit(solution)/shard_map/all_to_all | solution.py:127
  359.2 13.5 %all-to-all-start.5 = ((bf16[32,2,1536]{2,1,0:T(2,128)(2,1)}), bf16[32,2,1536]{2,1,0:T(2,128)(2,1)S(1)}, u32[]{:S(2)}, u32[]{:S(2)}) async-start(bf16[32,2,1536]{2,1,0:T(2,128)(2,1)} %reshape.208), calls=%async_computation.5 | async-start | bytes 393216 | tf_op jit(solution)/shard_map/all_to_all | solution.py:128
  372.8 13.5 %all-to-all-start.6 = ((bf16[32,2,1536]{2,1,0:T(2,128)(2,1)}), bf16[32,2,1536]{2,1,0:T(2,128)(2,1)S(1)}, u32[]{:S(2)}, u32[]{:S(2)}) async-start(bf16[32,2,1536]{2,1,0:T(2,128)(2,1)} %reshape.210), calls=%async_computation.6 | async-start | bytes 393216 | tf_op jit(solution)/shard_map/all_to_all | solution.py:129
  386.3 13.5 %all-to-all-start.7 = ((bf16[32,2,1536]{2,1,0:T(2,128)(2,1)}), bf16[32,2,1536]{2,1,0:T(2,128)(2,1)S(1)}, u32[]{:S(2)}, u32[]{:S(2)}) async-start(bf16[32,2,1536]{2,1,0:T(2,128)(2,1)} %reshape.212), calls=%async_computation.7 | async-start | bytes 393216 | tf_op jit(solution)/shard_map/all_to_all | solution.py:126
  392.1 303.6 %all-reduce.5.cloned.1.call-start = ((), (), s32[]{:S(2)}) async-start(), calls=%async_computation.8 | async-start | bytes 18874368
  396.3 7.3 %copy-start.2 = (bf16[4,32,768]{2,1,0:T(8,128)(2,1)S(1)}, bf16[4,32,768]{2,1,0:T(8,128)(2,1)}, u32[]{:S(2)}) copy-start(bf16[4,32,768]{2,1,0:T(8,128)(2,1)} %param.5) | copy-start | bytes 589828
  418.2 1.0 copy-start.3
Sparse Core Ops, SparseCore 0:
  73.1 263.0 all-reduce.6
  418.4 277.2 all-reduce.4
where the time goes:
time: 705 us; the launch traced here: 704 us
  waiting for transfers between devices  578 us (82%)
  starting transfers between devices  50.2 us (7%)
  other arithmetic  24 us (3%)
  matrix products  22 us (3%)
  local copies, waits for them, and re-layouts  15.4 us (2%)
  between operations  14.5 us (2%)
    unnamed x3, waiting for transfers between devices  276 us
    psum x1, waiting for transfers between devices, attend(): lax.psum(jnp.einsum('rchd,schd->hrs', back4, values4, preferred_element_t...  263 us
  transfers between devices with their start and end apart: 10, of which 10 were waited for; matrix products, arithmetic and copies ran while one was open for 3% of the time, Pallas kernels for 0%

commit v1 on v0

--- a/solution.py
+++ b/solution.py
@@ -53,10 +53,9 @@
     expon = jnp.exp(logits)
     probs = expon / jnp.sum(expon, -1, keepdims=True)
     probs_b = probs.astype(jnp.bfloat16)
-    slopes = lax.psum(
-        jnp.einsum("rchd,schd->hrs", back4, values4, preferred_element_type=jnp.float32),
-        ("read", "pos"),
-    )
+    piece_in = jnp.einsum("rchd,schd->hrs", back4, values4, preferred_element_type=jnp.float32)
+    latest = jax.lax.psum(piece_in, "pos")
+    slopes = jax.lax.psum(latest, "read")
     mixed = (scale * probs * (slopes - jnp.sum(probs * slopes, -1, keepdims=True))).astype(
         jnp.bfloat16
     )

time: 705 us -> 1070 us (1.52)
  waiting for transfers between devices: 578 us -> 923 us
  starting transfers between devices: 50.2 us -> 66.2 us
    psum x1 -> x3, waiting for transfers between devices: 263 us -> 614 us  [the longest x1 270 us: attend(): logits = lax.psum(partial_logits, ('read', 'pos')) * scale]
    all_to_all x1, starting transfers between devices: 5.76 us -> 20.8 us  [shards(): lax.all_to_all(output, 'read', split_axis=0, concat_axis=1, tiled=True)]
    unnamed x3 -> x5, waiting for transfers between devices: 276 us -> 279 us
  transfers between devices with their start and end apart: 10 -> 12, of which waited for: 10 -> 11; matrix products, arithmetic and copies ran while one was open for 3% -> 4% of each run, Pallas kernels for 0% -> 0%
where the time goes in v1:
time: 1070 us
  waiting for transfers between devices  923 us (86%)
  starting transfers between devices  66.2 us (6%)
  other arithmetic  24.1 us (2%)
  matrix products  22.5 us (2%)
  local copies, waits for them, and re-layouts  17.7 us (2%)
  between operations  14.2 us (1%)
    unnamed x5, waiting for transfers between devices  279 us
    psum x1, waiting for transfers between devices, attend(): logits = lax.psum(partial_logits, ('read', 'pos')) * scale  270 us
    psum x1, waiting for transfers between devices, attend(): slopes = jax.lax.psum(latest, 'read')  252 us
    psum x1, waiting for transfers between devices, attend(): latest = jax.lax.psum(piece_in, 'pos')  92.8 us
  transfers between devices with their start and end apart: 12, of which 11 were waited for; matrix products, arithmetic and copies ran while one was open for 4% of the time, Pallas kernels for 0%

profile of v1, /device:TPU:97, one launch (start us, length us, event | category | flops | bytes accessed | tf_op | source)
XLA Modules:
  0.0 1068.0 jit_solution(5765818076839455438)
XLA Ops:
  8.1 1.8 fusion.13
  10.7 8.1 all-to-all-start.2
  22.5 1.6 fusion.22
  25.0 1.6 all-to-all-done.2
  26.6 6.1 all-to-all-start.3
  32.7 1.6 fusion.16
  35.8 4.6 all-to-all-done.3
  40.5 5.8 all-to-all-start
  48.2 1.6 fusion.19
  50.7 3.3 all-to-all-done
  54.0 5.8 all-to-all-start.1
  60.5 10.1 all-to-all-done.1
  72.6 92.8 %all-reduce.8.cloned.1.call-done = f32[12,128,128]{2,1,0:T(8,128)} async-done(((f32[12,128,128]{2,1,0:T(8,128)}), f32[12,128,128]{2,1,0:T(8,128)}) %all-reduce.8.cloned.1.call-update) | async-done | bytes 786448 | tf_op jit(solution)/shard_map/psum | solution.py:57
  165.4 269.7 %all-reduce.6.cloned.1.call-done = f32[12,128,128]{2,1,0:T(8,128)} async-done(((f32[12,128,128]{2,1,0:T(8,128)}), f32[12,128,128]{2,1,0:T(8,128)}) %all-reduce.6.cloned.1.call-update) | async-done | bytes 786448 | tf_op jit(solution)/shard_map/psum | solution.py:52
  436.6 1.6 fusion.25
  440.4 7.4 all-to-all-start.6
  450.1 251.9 %all-reduce.10.cloned.1.call-done = f32[12,128,128]{2,1,0:T(8,128)} async-done(((f32[12,128,128]{2,1,0:T(8,128)}), f32[12,128,128]{2,1,0:T(8,128)}) %all-reduce.10.cloned.1.call-update) | async-done | bytes 786448 | tf_op jit(solution)/shard_map/psum | solution.py:58
  702.0 1.6 multiply_reduce_fusion
  703.6 20.8 %all-to-all-start.7 = ((bf16[32,2,1536]{2,1,0:T(2,128)(2,1)}), bf16[32,2,1536]{2,1,0:T(2,128)(2,1)S(1)}, u32[]{:S(2)}, u32[]{:S(2)}) async-start(bf16[32,2,1536]{2,1,0:T(2,128)(2,1)} %reshape.212), calls=%async_computation.7 | async-start | bytes 393216 | tf_op jit(solution)/shard_map/all_to_all | solution.py:125
  724.4 1.6 multiply_convert_fusion
  728.1 4.1 all-to-all-done.7
  732.2 5.8 all-to-all-start.4
  741.4 4.3 all-to-all-done.4
  745.7 6.3 all-to-all-start.5
  755.4 2.6 fusion.7
  758.0 1.8 all-to-all-done.5
  761.4 1.8 reduce.2
  764.2 1.9 convolution_add_fusion.1
  766.1 1.9 fusion.42
  768.1 4.0 fusion.36
  772.0 8.1 pad_maximum_fusion
  781.0 278.9 %all-reduce.12.cloned.1.call-done = f32[768,3072]{1,0:T(8,128)} async-done(((f32[768,3072]{1,0:T(8,128)}), f32[768,3072]{1,0:T(8,128)}) %all-reduce.12.cloned.1.call-update) | async-done | bytes 9437200
  (79 shorter events, 33.0 us)
Async XLA Ops:
  7.2 0.9 copy-start
  10.7 15.8 %all-to-all-start.2 = ((bf16[4,32,768]{2,0,1:T(4,128)(2,1)}), bf16[4,32,768]{2,0,1:T(4,128)(2,1)S(1)}, u32[]{:S(2)}, u32[]{:S(2)}) async-start(bf16[4,32,768]{2,0,1:T(4,128)(2,1)} %copy.37), calls=%async_computation.2 | async-start | bytes 393216 | tf_op jit(solution)/shard_map/all_to_all | solution.py:117
  26.6 13.9 %all-to-all-start.3 = ((bf16[4,32,768]{2,0,1:T(4,128)(2,1)}), bf16[4,32,768]{2,0,1:T(4,128)(2,1)S(1)}, u32[]{:S(2)}, u32[]{:S(2)}) async-start(bf16[4,32,768]{2,0,1:T(4,128)(2,1)} %copy.38), calls=%async_computation.3 | async-start | bytes 393216 | tf_op jit(solution)/shard_map/all_to_all | solution.py:114
  40.5 13.5 %all-to-all-start = ((bf16[4,32,768]{2,0,1:T(4,128)(2,1)}), bf16[4,32,768]{2,0,1:T(4,128)(2,1)S(1)}, u32[]{:S(2)}, u32[]{:S(2)}) async-start(bf16[4,32,768]{2,0,1:T(4,128)(2,1)} %copy.33), calls=%async_computation | async-start | bytes 393216 | tf_op jit(solution)/shard_map/all_to_all | solution.py:113
  46.2 119.1 %all-reduce.8.cloned.1.call-start = ((), (), s32[]{:S(2)}) async-start(), calls=%async_computation.9 | async-start | bytes 1572864 | tf_op jit(solution)/shard_map/psum | solution.py:57
  48.2 117.2 %copy-start.3 = (s32[128]{0:T(128)S(1)}, s32[128]{0:T(128)}, u32[]{:S(2)}) copy-start(s32[128]{0:T(128)} %param.9) | copy-start | bytes 1540
  48.2 117.2 %copy-start.4 = (s32[128]{0:T(128)S(1)}, s32[128]{0:T(128)}, u32[]{:S(2)}) copy-start(s32[128]{0:T(128)} %param.8) | copy-start | bytes 1540
  54.0 16.6 %all-to-all-start.1 = ((bf16[4,32,768]{2,0,1:T(4,128)(2,1)}), bf16[4,32,768]{2,0,1:T(4,128)(2,1)S(1)}, u32[]{:S(2)}, u32[]{:S(2)}) async-start(bf16[4,32,768]{2,0,1:T(4,128)(2,1)} %copy.34), calls=%async_computation.1 | async-start | bytes 393216 | tf_op jit(solution)/shard_map/all_to_all | solution.py:112
  59.8 375.3 %all-reduce.6.cloned.1.call-start = ((), (), s32[]{:S(2)}) async-start(), calls=%async_computation.8 | async-start | bytes 1572864 | tf_op jit(solution)/shard_map/psum | solution.py:52
  72.6 629.4 %all-reduce.10.cloned.1.call-start = ((), (), s32[]{:S(2)}) async-start(), calls=%async_computation.10 | async-start | bytes 1572864 | tf_op jit(solution)/shard_map/psum | solution.py:58
  435.1 12.8 %copy-start.1 = (f32[12,128,128]{2,1,0:T(8,128)S(1)}, f32[12,128,128]{2,1,0:T(8,128)}, u32[]{:S(2)}) copy-start(f32[12,128,128]{2,1,0:T(8,128)} %all-reduce.6.cloned.1.call-done) | copy-start | bytes 2359300
  440.4 263.2 %all-to-all-start.6 = ((bf16[32,2,1536]{2,1,0:T(2,128)(2,1)}), bf16[32,2,1536]{2,1,0:T(2,128)(2,1)S(1)}, u32[]{:S(2)}, u32[]{:S(2)}) async-start(bf16[32,2,1536]{2,1,0:T(2,128)(2,1)} %reshape.210), calls=%async_computation.6 | async-start | bytes 393216 | tf_op jit(solution)/shard_map/all_to_all | solution.py:128
  703.6 28.6 %all-to-all-start.7 = ((bf16[32,2,1536]{2,1,0:T(2,128)(2,1)}), bf16[32,2,1536]{2,1,0:T(2,128)(2,1)S(1)}, u32[]{:S(2)}, u32[]{:S(2)}) async-start(bf16[32,2,1536]{2,1,0:T(2,128)(2,1)} %reshape.212), calls=%async_computation.7 | async-start | bytes 393216 | tf_op jit(solution)/shard_map/all_to_all | solution.py:125
  732.2 13.5 %all-to-all-start.4 = ((bf16[32,2,1536]{2,1,0:T(2,128)(2,1)}), bf16[32,2,1536]{2,1,0:T(2,128)(2,1)S(1)}, u32[]{:S(2)}, u32[]{:S(2)}) async-start(bf16[32,2,1536]{2,1,0:T(2,128)(2,1)} %reshape.206), calls=%async_computation.4 | async-start | bytes 393216 | tf_op jit(solution)/shard_map/all_to_all | solution.py:126
  745.7 14.1 %all-to-all-start.5 = ((bf16[32,2,1536]{2,1,0:T(2,128)(2,1)}), bf16[32,2,1536]{2,1,0:T(2,128)(2,1)}, u32[]{:S(2)}, u32[]{:S(2)}) async-start(bf16[32,2,1536]{2,1,0:T(2,128)(2,1)} %reshape.208), calls=%async_computation.5 | async-start | bytes 393216 | tf_op jit(solution)/shard_map/all_to_all | solution.py:127
  752.1 307.8 %all-reduce.12.cloned.1.call-start = ((), (), s32[]{:S(2)}) async-start(), calls=%async_computation.11 | async-start | bytes 18874368
  752.8 13.4 %copy-start.2 = (bf16[4,32,768]{2,1,0:T(8,128)(2,1)S(1)}, bf16[4,32,768]{2,1,0:T(8,128)(2,1)}, u32[]{:S(2)}) copy-start(bf16[4,32,768]{2,1,0:T(8,128)(2,1)} %param.5) | copy-start | bytes 589828
Sparse Core Ops, SparseCore 0:
  49.7 115.6 all-reduce.7
  170.8 264.2 all-reduce.5
  437.7 264.1 all-reduce.9
  780.2 279.6 all-reduce.11
